TPU v7x, 256 devices: a whole 4x4x8 slice. The times are simulated.
256 devices in a mesh: gx: 32 (over z, x_hi, core), gy: 8 (over x_lo, y).
Axes of the slice: x: 4 (x_hi: 2, x_lo: 2; x = x_hi * 2 + x_lo), y: 4, z: 8, core: 2. Of those that a mesh axis runs over, the one named last changes fastest.
Arguments:
- conc: float32 [32, 2048, 1024], P(None, 'gx', 'gy'), may hold values from -4 to 4
- mobility: float32 [32, 2048, 1024], P(None, 'gx', 'gy'), may hold values from 0.3 to 3
- block_x: float32 [32, 2048, 64], P(None, 'gx'), may hold values from -0.75 to 0.75
- spike_x: float32 [32, 2048, 4], P(None, 'gx'), may hold values from -3 to 3
- reduced_x: float32 [32, 128, 128], replicated, may hold values from -0.5 to 0.5
- block_y: float32 [32, 1024, 128], P(None, 'gy'), may hold values from -0.5 to 0.5
- spike_y: float32 [32, 1024, 4], P(None, 'gy'), may hold values from -3 to 3
- reduced_y: float32 [32, 32, 32], replicated, may hold values from -1 to 1
Outputs:
- conc_next: float32 [32, 2048, 1024], P(None, 'gx', 'gy')
All inputs are finite; a program needn't handle non-finite values.
Results may differ from a plain program's by a relative error of at most 0.00012.
Values sent between devices are 32-bit elements; how exact they have to be, the bound alone decides.
No kernel may reach another device: no remote copies, remote signals or barrier semaphores. Data moves between devices by JAX's collectives and lax.ppermute only.
A program may use at most 64 MiB of HBM per device.

v0:
```python
import jax
import jax.numpy as jnp
from jax import lax
from jax.sharding import PartitionSpec as P

HIGH = lax.Precision.HIGHEST


def extended_2(shard, sides, width):
    for axis, dim in sides:
        devices, length = (lax.axis_size(axis), shard.shape[dim])
        up = [(i, (i + 1) % devices) for i in range(devices)]
        down = [(j, i) for i, j in up]
        last = lax.slice_in_dim(shard, length - width, length, axis=dim)
        leading = lax.slice_in_dim(shard, 0, width, axis=dim)
        before = lax.ppermute(last, axis, up)
        after = lax.ppermute(leading, axis, down)
        shard = jnp.concatenate([before, shard, after], axis=dim)
    return shard


def divergence(conc, mu_ext, mob_ext):
    mu_mid = mu_ext[:, 1:-1, 1:-1]
    mob_mid = mob_ext[:, 1:-1, 1:-1]
    total = jnp.zeros_like(conc)
    for lo_x, hi_x, lo_y, hi_y in (
        (2, None, 1, -1),
        (0, -2, 1, -1),
        (1, -1, 2, None),
        (1, -1, 0, -2),
    ):
        mu_side = mu_ext[:, lo_x:hi_x, lo_y:hi_y]
        mob_side = mob_ext[:, lo_x:hi_x, lo_y:hi_y]
        total = total + 0.5 * (mob_side + mob_mid) * (mu_side - mu_mid)
    return conc + 0.02 * total


def laplace(padded):
    return (
        padded[:, 2:, 1:-1]
        + padded[:, :-2, 1:-1]
        + padded[:, 1:-1, 2:]
        + padded[:, 1:-1, :-2]
        - 4.0 * padded[:, 1:-1, 1:-1]
    )


def potential(centre, lap):
    return centre * centre * centre - centre - 1.0 * lap


def mobile(prefactor, centre):
    sq = centre * centre
    return prefactor * (0.25 + sq) / (1.0 + sq)


def solve_x(field, block_x, spike_x, reduced_x):
    width = field.shape[1]
    lin = jnp.einsum("zij,zjn->zin", block_x, field, precision=HIGH)
    rims = jnp.concatenate([lin[:, 0:2], lin[:, width - 2 :]], axis=1)
    whole = reduced_x.shape[1]
    place = lax.axis_index("gx")
    gathered = lax.all_gather(rims, "gx", axis=1, tiled=True)
    offsets = jnp.array([-2, -1, 4, 5], jnp.int32)
    picks = (4 * place + offsets) % whole
    rows_used = jnp.take(reduced_x, picks, axis=1)
    coupled = jnp.einsum("zrk,zkn->zrn", rows_used, gathered, precision=HIGH)
    return lin - jnp.einsum("zik,zkn->zin", spike_x, coupled, precision=HIGH)


def solve_y(field, block_y, spike_y, reduced_y):
    width = field.shape[2]
    lin = jnp.einsum("zij,zxj->zxi", block_y, field, precision=HIGH)
    rims = jnp.transpose(
        jnp.concatenate([lin[:, :, 0:2], lin[:, :, width - 2 :]], axis=2), (0, 2, 1)
    )
    gathered = lax.all_gather(rims, "gy", axis=1, tiled=True)
    whole = reduced_y.shape[1]
    place = lax.axis_index("gy")
    offsets = jnp.array([-2, -1, 4, 5], jnp.int32)
    picks = (4 * place + offsets) % whole
    rows_used = jnp.take(reduced_y, picks, axis=1)
    coupled = jnp.einsum("zrk,zkx->zrx", rows_used, gathered, precision=HIGH)
    return lin - jnp.einsum("zik,zkx->zxi", spike_y, coupled, precision=HIGH)


def body(conc, mobility, block_x, spike_x, reduced_x, block_y, spike_y, reduced_y):
    padded = extended_2(conc, (("gx", 1), ("gy", 2)), 1)
    mu_here = potential(conc, laplace(padded))
    mob_here = mobile(mobility, conc)
    extended = extended_2(jnp.stack([mu_here, mob_here]), (("gx", 2), ("gy", 3)), 1)
    rhs = divergence(conc, extended[0], extended[1])
    xsol = solve_x(rhs, block_x, spike_x, reduced_x)
    return solve_y(xsol, block_y, spike_y, reduced_y)


def solution(mesh):
    in_specs = (
        P(None, "gx", "gy"),
        P(None, "gx", "gy"),
        P(None, "gx", None),
        P(None, "gx", None),
        P(),
        P(None, "gy", None),
        P(None, "gy", None),
        P(),
    )
    out_specs = P(None, "gx", "gy")
    return jax.shard_map(body, mesh=mesh, in_specs=in_specs, out_specs=out_specs, check_vma=False)
```

profile of v0, /device:TPU:24, one launch (start us, length us, event | category | flops | bytes accessed | tf_op | source)
XLA Modules:
  0.0 214.3 jit_solution(208142378381438117)
XLA Ops:
  7.7 7.8 %collective-permute-start = (f32[32,1,128]{2,0,1:T(8,128)S(1)}, f32[32,1,128]{2,0,1:T(8,128)S(1)}, u32[]{:S(2)}, u32[]{:S(2)}) collective-permute-start(f32[32,1,128]{2,0,1:T(8,128)S(1)} %bitcast.50), channel_id=1, source_target_pairs={{8,0},{16,8},{24,16},{32,24},{40,32},{48,40},{56,48},{64,56},{72,6... | collective-permute-start | bytes 49160 | tf_op jit(solution)/shard_map/ppermute | solution.py:17
  15.5 1.4 collective-permute-done
  17.0 5.3 %collective-permute-done.1 = f32[32,1,128]{2,0,1:T(8,128)S(1)} collective-permute-done((f32[32,1,128]{2,0,1:T(8,128)S(1)}, f32[32,1,128]{2,0,1:T(8,128)S(1)}, u32[]{:S(2)}, u32[]{:S(2)}) %collective-permute-start.1) | collective-permute-done | bytes 16416 | tf_op jit(solution)/shard_map/ppermute | solution.py:16
  22.3 1.3 pad_maximum_fusion.2
  23.6 1.4 fusion.54
  25.1 1.7 copy.61
  28.0 3.4 %collective-permute-start.3 = (f32[32,66,1]{1,0,2:T(8,128)S(1)}, f32[32,66,1]{1,0,2:T(8,128)S(1)}, u32[]{:S(2)}, u32[]{:S(2)}) collective-permute-start(f32[32,66,1]{1,0,2:T(8,128)S(1)} %copy.63), channel_id=1, source_target_pairs={{0,1},{1,2},{2,3},{3,4},{4,5},{5,6},{6,7},{7,0},{8,9},{9,10},{10,1... | collective-permute-start | bytes 25352 | tf_op jit(solution)/shard_map/ppermute | solution.py:16
  32.6 1.5 copy.62
  34.2 1.5 copy.64
  35.7 5.3 %fusion.7 = (f32[1,32,64,128]{3,2,1,0:T(8,128)S(1)}, f32[1,32,64,128]{3,2,1,0:T(8,128)S(1)}) fusion(f32[32,64,128]{2,1,0:T(8,128)} %param.10, f32[32,66,1]{2,1,0:T(8,128)} %copy.64, f32[32,1,128]{2,1,0:T(1,128)S(1)} %bitcast.44, f32[32,1,128]{2,1,0:T(1,128)S(1)} %bitcast.46, f32[32,66,1]{2,1,0:T(8,128)} %copy.62, f32[32,64,128]{2,1,0:T(8,128)} %param.11), kind=kLoop, calls=%fused_computation.20 | loop fusion | flops 5505024 | bytes 4243968 | tf_op jit(solution)/shard_map/stack | solution.py:91
  41.2 5.3 %collective-permute-start.5 = (f32[2,32,1,128]{3,1,2,0:T(8,128)S(1)}, f32[2,32,1,128]{3,1,2,0:T(8,128)S(1)}, u32[]{:S(2)}, u32[]{:S(2)}) collective-permute-start(f32[2,32,1,128]{3,1,2,0:T(8,128)S(1)} %bitcast.47), channel_id=1, source_target_pairs={{8,0},{16,8},{24,16},{32,24},{40,32},{48,40},{56,48},{64,56},{72,6... | collective-permute-start | bytes 98312 | tf_op jit(solution)/shard_map/ppermute | solution.py:17
  46.5 1.6 collective-permute-done.4
  48.5 2.9 %fusion.53 = (f32[2,32,66,1]{3,2,1,0:T(8,128)}, f32[2,32,66,1]{3,2,1,0:T(8,128)}) fusion(f32[2,32,66,128]{3,2,1,0:T(8,128)S(1)} %pad_maximum_fusion.1), kind=kLoop, calls=%fused_computation.90 | loop fusion | bytes 67584 | tf_op jit(solution)/shard_map/slice | solution.py:14
  51.4 2.4 %copy.69 = f32[2,32,66,1]{2,1,3,0:T(8,128)S(1)} copy(f32[2,32,66,1]{3,2,1,0:T(8,128)} %get-tuple-element.11) | data formatting | bytes 33792 | tf_op jit(solution)/shard_map/slice | solution.py:14
  53.8 3.2 %collective-permute-start.6 = (f32[2,32,66,1]{2,1,3,0:T(8,128)S(1)}, f32[2,32,66,1]{2,1,3,0:T(8,128)S(1)}, u32[]{:S(2)}, u32[]{:S(2)}) collective-permute-start(f32[2,32,66,1]{2,1,3,0:T(8,128)S(1)} %copy.69), channel_id=1, source_target_pairs={{0,1},{1,2},{2,3},{3,4},{4,5},{5,6},{6,7},{7,0},{8,9},{9,10},{10,1... | collective-permute-start | bytes 50696 | tf_op jit(solution)/shard_map/ppermute | solution.py:16
  57.0 2.4 %copy.70 = f32[2,32,66,1]{2,1,3,0:T(8,128)S(1)} copy(f32[2,32,66,1]{3,2,1,0:T(8,128)} %get-tuple-element.12) | data formatting | bytes 33792 | tf_op jit(solution)/shard_map/slice | solution.py:15
  59.7 2.3 %copy.71 = f32[2,32,66,1]{3,2,1,0:T(8,128)} copy(f32[2,32,66,1]{2,1,3,0:T(8,128)S(1)} %collective-permute-done.6) | data formatting | bytes 33792 | tf_op jit(solution)/shard_map/ppermute | solution.py:16
  62.0 3.7 %collective-permute-done.7 = f32[2,32,66,1]{2,1,3,0:T(8,128)S(1)} collective-permute-done((f32[2,32,66,1]{2,1,3,0:T(8,128)S(1)}, f32[2,32,66,1]{2,1,3,0:T(8,128)S(1)}, u32[]{:S(2)}, u32[]{:S(2)}) %collective-permute-start.7) | collective-permute-done | bytes 16928 | tf_op jit(solution)/shard_map/ppermute | solution.py:17
  65.7 2.3 %copy.72 = f32[2,32,66,1]{3,2,1,0:T(8,128)} copy(f32[2,32,66,1]{2,1,3,0:T(8,128)S(1)} %collective-permute-done.7) | data formatting | bytes 33792 | tf_op jit(solution)/shard_map/ppermute | solution.py:17
  68.0 5.2 %pad_maximum_fusion = f32[2,32,66,130]{3,2,1,0:T(8,128)S(1)} fusion(f32[2,32,66,1]{3,2,1,0:T(8,128)} %copy.72, f32[2,32,1,128]{3,2,1,0:T(1,128)S(1)} %bitcast.42, f32[1,32,64,128]{3,2,1,0:T(8,128)} %copy-done.1, f32[1,32,64,128]{3,2,1,0:T(8,128)S(1)} %get-tuple-element.21, f32[2,32,1,128]{3,2,1,0:T(1,128)S(1)} %bitcast.40, f32[2,32,66,1]{3,2,1,0:T(8,128)} %copy.71), kind=kLoop, calls=%fused_computation.2 | loop fusion | flops 2745600 | bytes 4392960 | tf_op jit(solution)/shard_map/concatenate | solution.py:18
  74.4 5.3 %convolution_bitcast_fusion.1 = f32[32,64,128]{2,1,0:T(8,128)} fusion(f32[32,64,64]{2,1,0:T(8,128)} %param.12, f32[32,64,128]{2,1,0:T(8,128)S(1)} %copy-done.2, f32[32,66,130]{2,1,0:T(8,128)S(1)} %get-tuple-element.10, f32[32,66,130]{2,1,0:T(8,128)S(1)} %get-tuple-element.9), kind=kOutput, calls=%fused_computation.14 | convolution fusion | flops 206831616 | bytes 13107200 | tf_op jit(solution)/shard_map/zij,zjn->zin/dot_general | solution.py:59
  81.6 1.6 gather_fusion
  83.2 1.7 gather_fusion.1
  84.9 74.2 %all-gather.2.cloned.1.call-done = f32[32,128,128]{2,0,1:T(8,128)} async-done(((f32[32,4,128]{2,0,1:T(8,128)}), f32[32,128,128]{2,0,1:T(8,128)}) %all-gather.2.cloned.1.call-update) | async-done | bytes 2097168 | tf_op jit(solution)/shard_map/all_gather | solution.py:63
  159.1 4.4 %fusion = f32[32,4,128]{2,1,0:T(4,128)S(1)} fusion(f32[32,128,128]{2,0,1:T(8,128)} %all-gather.2.cloned.1.call-done, f32[4,32,128]{2,0,1:T(4,128)S(1)} %gather_fusion, pred[4]{0:T(512)(128)(4,1)S(1)} %get-tuple-element.25), kind=kOutput, calls=%fused_computation.6 | convolution fusion | flops 25182208 | bytes 2228228 | tf_op jit(solution)/shard_map/zrk,zkn->zrn/dot_general | solution.py:67
  163.4 1.8 fusion.2
  165.3 4.1 %fusion.58 = f32[32,64,128]{2,1,0:T(8,128)S(1)} fusion(f32[32,64,128]{2,1,0:T(8,128)S(1)} %fusion.2, f32[32,128,128]{2,1,0:T(8,128)S(1)} %copy-done), kind=kOutput, calls=%fused_computation.95 | convolution fusion | flops 402653184 | bytes 4194304 | tf_op jit(solution)/shard_map/zij,zxj->zxi/dot_general | solution.py:73
  169.4 1.7 fusion.55
  171.2 1.6 copy.75
  172.8 1.6 copy.76
  174.4 29.4 %all_gather.7 = f32[32,32,64]{2,0,1:T(8,128)S(1)} all-gather(f32[32,4,64]{2,0,1:T(8,128)S(1)} %maximum_bitcast_fusion), channel_id=1, replica_groups=mesh['gx'=32,'gy'=8] {'gy'}, dimensions={1}, use_global_device_ids=true | all-gather | bytes 294912 | tf_op jit(solution)/shard_map/all_gather | solution.py:77
  204.6 2.8 %convolution_subtract_fusion = f32[32,64,128]{2,1,0:T(8,128)} fusion(f32[32,64,128]{2,1,0:T(8,128)S(1)} %fusion.58, f32[32,4,64]{2,1,0:T(4,128)S(1)} %fusion.35, f32[32,128,4]{1,2,0:T(4,128)S(1)} %copy-done.5), kind=kOutput, calls=%fused_computation.11 | convolution fusion | flops 12845056 | bytes 2195456 | tf_op jit(solution)/shard_map/zik,zkx->zxi/dot_general | solution.py:84
  (37 shorter events, 8.2 us)
Async XLA Ops:
  6.5 158.7 %copy-start = (f32[32,128,128]{2,1,0:T(8,128)S(1)}, f32[32,128,128]{2,1,0:T(8,128)}, u32[]{:S(2)}) copy-start(f32[32,128,128]{2,1,0:T(8,128)} %param.15) | copy-start | bytes 6291460
  6.5 152.5 %all-gather.2.cloned.1.call-start = ((), (), s32[]{:S(2)}) async-start(), calls=%async_computation | async-start | bytes 2162688 | tf_op jit(solution)/shard_map/all_gather | solution.py:63
  7.7 9.3 %collective-permute-start = (f32[32,1,128]{2,0,1:T(8,128)S(1)}, f32[32,1,128]{2,0,1:T(8,128)S(1)}, u32[]{:S(2)}, u32[]{:S(2)}) collective-permute-start(f32[32,1,128]{2,0,1:T(8,128)S(1)} %bitcast.50), channel_id=1, source_target_pairs={{8,0},{16,8},{24,16},{32,24},{40,32},{48,40},{56,48},{64,56},{72,6... | collective-permute-start | bytes 49160 | tf_op jit(solution)/shard_map/ppermute | solution.py:17
  15.5 6.8 %collective-permute-start.1 = (f32[32,1,128]{2,0,1:T(8,128)S(1)}, f32[32,1,128]{2,0,1:T(8,128)S(1)}, u32[]{:S(2)}, u32[]{:S(2)}) collective-permute-start(f32[32,1,128]{2,0,1:T(8,128)S(1)} %bitcast.49), channel_id=1, source_target_pairs={{0,8},{8,16},{16,24},{24,32},{32,40},{40,48},{48,56},{56,64},{64,7... | collective-permute-start | bytes 49160 | tf_op jit(solution)/shard_map/ppermute | solution.py:16
  26.7 5.9 %collective-permute-start.2 = (f32[32,66,1]{1,0,2:T(8,128)S(1)}, f32[32,66,1]{1,0,2:T(8,128)S(1)}, u32[]{:S(2)}, u32[]{:S(2)}) collective-permute-start(f32[32,66,1]{1,0,2:T(8,128)S(1)} %copy.61), channel_id=1, source_target_pairs={{1,0},{2,1},{3,2},{4,3},{5,4},{6,5},{7,6},{0,7},{9,8},{10,9},{11,1... | collective-permute-start | bytes 25352 | tf_op jit(solution)/shard_map/ppermute | solution.py:17
  28.0 6.2 %collective-permute-start.3 = (f32[32,66,1]{1,0,2:T(8,128)S(1)}, f32[32,66,1]{1,0,2:T(8,128)S(1)}, u32[]{:S(2)}, u32[]{:S(2)}) collective-permute-start(f32[32,66,1]{1,0,2:T(8,128)S(1)} %copy.63), channel_id=1, source_target_pairs={{0,1},{1,2},{2,3},{3,4},{4,5},{5,6},{6,7},{7,0},{8,9},{9,10},{10,1... | collective-permute-start | bytes 25352 | tf_op jit(solution)/shard_map/ppermute | solution.py:16
  41.0 7.5 %copy-start.1 = (f32[1,32,64,128]{3,2,1,0:T(8,128)}, f32[1,32,64,128]{3,2,1,0:T(8,128)S(1)}, u32[]{:S(2)}) copy-start(f32[1,32,64,128]{3,2,1,0:T(8,128)S(1)} %get-tuple-element.22) | copy-start | bytes 3145732
  41.1 7.0 %collective-permute-start.4 = (f32[2,32,1,128]{3,1,2,0:T(8,128)S(1)}, f32[2,32,1,128]{3,1,2,0:T(8,128)S(1)}, u32[]{:S(2)}, u32[]{:S(2)}) collective-permute-start(f32[2,32,1,128]{3,1,2,0:T(8,128)S(1)} %bitcast.48), channel_id=1, source_target_pairs={{0,8},{8,16},{16,24},{24,32},{32,40},{40,48},{48,56},{56,64},{64,7... | collective-permute-start | bytes 98312 | tf_op jit(solution)/shard_map/ppermute | solution.py:16
  41.2 6.9 %collective-permute-start.5 = (f32[2,32,1,128]{3,1,2,0:T(8,128)S(1)}, f32[2,32,1,128]{3,1,2,0:T(8,128)S(1)}, u32[]{:S(2)}, u32[]{:S(2)}) collective-permute-start(f32[2,32,1,128]{3,1,2,0:T(8,128)S(1)} %bitcast.47), channel_id=1, source_target_pairs={{8,0},{16,8},{24,16},{32,24},{40,32},{48,40},{56,48},{64,56},{72,6... | collective-permute-start | bytes 98312 | tf_op jit(solution)/shard_map/ppermute | solution.py:17
  53.8 5.9 %collective-permute-start.6 = (f32[2,32,66,1]{2,1,3,0:T(8,128)S(1)}, f32[2,32,66,1]{2,1,3,0:T(8,128)S(1)}, u32[]{:S(2)}, u32[]{:S(2)}) collective-permute-start(f32[2,32,66,1]{2,1,3,0:T(8,128)S(1)} %copy.69), channel_id=1, source_target_pairs={{0,1},{1,2},{2,3},{3,4},{4,5},{5,6},{6,7},{7,0},{8,9},{9,10},{10,1... | collective-permute-start | bytes 50696 | tf_op jit(solution)/shard_map/ppermute | solution.py:16
  59.4 6.3 %collective-permute-start.7 = (f32[2,32,66,1]{2,1,3,0:T(8,128)S(1)}, f32[2,32,66,1]{2,1,3,0:T(8,128)S(1)}, u32[]{:S(2)}, u32[]{:S(2)}) collective-permute-start(f32[2,32,66,1]{2,1,3,0:T(8,128)S(1)} %copy.70), channel_id=1, source_target_pairs={{1,0},{2,1},{3,2},{4,3},{5,4},{6,5},{7,6},{0,7},{9,8},{10,9},{11,1... | collective-permute-start | bytes 50696 | tf_op jit(solution)/shard_map/ppermute | solution.py:17
  73.2 1.2 copy-start.2
  74.4 7.1 %copy-start.6 = (s32[4]{0:T(128)S(1)}, s32[4]{0:T(128)}, u32[]{:S(2)}) copy-start(s32[4]{0:T(128)} %constant.74.clone) | copy-start | bytes 52
  79.7 83.7 %copy-start.3 = (f32[32,64,128]{2,1,0:T(8,128)S(1)}, f32[32,64,128]{2,1,0:T(8,128)}, u32[]{:S(2)}) copy-start(f32[32,64,128]{2,1,0:T(8,128)} %convolution_bitcast_fusion.1) | copy-start | bytes 3145732
  79.7 83.7 %copy-start.4 = (f32[32,64,4]{1,2,0:T(4,128)S(1)}, f32[32,64,4]{1,2,0:T(4,128)}, u32[]{:S(2)}) copy-start(f32[32,64,4]{1,2,0:T(4,128)} %param.13) | copy-start | bytes 98308
  171.2 33.5 %copy-start.5 = (f32[32,128,4]{1,2,0:T(4,128)S(1)}, f32[32,128,4]{1,2,0:T(4,128)}, u32[]{:S(2)}) copy-start(f32[32,128,4]{1,2,0:T(4,128)} %param.16) | copy-start | bytes 196612
Sparse Core Ops, SparseCore 0:
  81.7 77.3 all-gather.1
where the time goes:
time: 215 us; the launch traced here: 214 us
  waiting for transfers between devices  87.5 us (41%)
  local copies, waits for them, and re-layouts  31.3 us (15%)
  blocking collectives  29.4 us (14%)
  starting transfers between devices  20.9 us (10%)
  matrix products  19.3 us (9%)
  between operations  13.6 us (6%)
  other arithmetic  12.3 us (6%)
    all_gather x1, waiting for transfers between devices, solve_x(): gathered = lax.all_gather(rims, 'gx', axis=1, tiled=True)  74.2 us
    all_gather x1, blocking collectives, solve_y(): gathered = lax.all_gather(rims, 'gy', axis=1, tiled=True)  29.4 us
    ppermute x4, starting transfers between devices, extended_2(): after = lax.ppermute(leading, axis, down)  14.2 us
    ppermute x4, waiting for transfers between devices, extended_2(): before = lax.ppermute(last, axis, up)  6.93 us
    slice x4, local copies, waits for them, and re-layouts, extended_2(): last = lax.slice_in_dim(shard, length - width, length, axis=dim)  6.9 us
    concatenate x3, other arithmetic, extended_2(): shard = jnp.concatenate([before, shard, after], axis=dim)  6.88 us
    ppermute x4, starting transfers between devices, extended_2(): before = lax.ppermute(last, axis, up)  6.69 us
    ppermute x4, waiting for transfers between devices, extended_2(): after = lax.ppermute(leading, axis, down)  6.4 us
  transfers between devices with their start and end apart: 9, of which 6 were waited for; matrix products, arithmetic and copies ran while one was open for 5% of the time, Pallas kernels for 0%

commit v1 on v0

--- a/solution.py
+++ b/solution.py
@@ -74,7 +74,8 @@
     rims = jnp.transpose(
         jnp.concatenate([lin[:, :, 0:2], lin[:, :, width - 2 :]], axis=2), (0, 2, 1)
     )
-    gathered = lax.all_gather(rims, "gy", axis=1, tiled=True)
+    sent = jnp.stack([rims] * lax.axis_size("gy"))
+    gathered = jnp.concatenate(lax.all_to_all(sent, "gy", 0, 0), axis=1)
     whole = reduced_y.shape[1]
     place = lax.axis_index("gy")
     offsets = jnp.array([-2, -1, 4, 5], jnp.int32)

time: 215 us -> 206 us (0.958)
  blocking collectives: 29.4 us -> 0 us
  local copies, waits for them, and re-layouts: 31.3 us -> 36.6 us
  waiting for transfers between devices: 87.5 us -> 92.7 us
  starting transfers between devices: 20.9 us -> 25.7 us
  other arithmetic: 12.3 us -> 14.6 us
    all_gather x1 -> x0, blocking collectives: 29.4 us -> none  [solve_y(): gathered = lax.all_gather(rims, 'gy', axis=1, tiled=True)]
    unnamed x14 -> x19, local copies, waits for them, and re-layouts: 0.92 us -> 5.76 us
    all_to_all x0 -> x1, starting transfers between devices: none -> 4.79 us  [solve_y(): gathered = jnp.concatenate(lax.all_to_all(sent, 'gy', 0, 0), axis=1)]
    all_to_all x0 -> x1, waiting for transfers between devices: none -> 3.49 us  [solve_y(): gathered = jnp.concatenate(lax.all_to_all(sent, 'gy', 0, 0), axis=1)]
    all_to_all x0 -> x1, other arithmetic: none -> 2.24 us  [solve_y(): gathered = jnp.concatenate(lax.all_to_all(sent, 'gy', 0, 0), axis=1)]
  transfers between devices with their start and end apart: 9 -> 10, of which waited for: 6 -> 7; matrix products, arithmetic and copies ran while one was open for 5% -> 5% of each run, Pallas kernels for 0% -> 0%
where the time goes in v1:
time: 206 us; the launch traced here: 204 us
  waiting for transfers between devices  92.7 us (45%)
  local copies, waits for them, and re-layouts  36.6 us (18%)
  starting transfers between devices  25.7 us (12%)
  matrix products  20.3 us (10%)
  other arithmetic  14.6 us (7%)
  between operations  13.6 us (7%)
    all_gather x1, waiting for transfers between devices, solve_x(): gathered = lax.all_gather(rims, 'gx', axis=1, tiled=True)  75.9 us
    ppermute x4, starting transfers between devices, extended_2(): after = lax.ppermute(leading, axis, down)  14.2 us
    ppermute x4, waiting for transfers between devices, extended_2(): before = lax.ppermute(last, axis, up)  6.93 us
    slice x4, local copies, waits for them, and re-layouts, extended_2(): last = lax.slice_in_dim(shard, length - width, length, axis=dim)  6.89 us
    concatenate x3, other arithmetic, extended_2(): shard = jnp.concatenate([before, shard, after], axis=dim)  6.88 us
    ppermute x4, starting transfers between devices, extended_2(): before = lax.ppermute(last, axis, up)  6.69 us
    ppermute x4, waiting for transfers between devices, extended_2(): after = lax.ppermute(leading, axis, down)  6.4 us
    unnamed x19, local copies, waits for them, and re-layouts  5.76 us
  transfers between devices with their start and end apart: 10, of which 7 were waited for; matrix products, arithmetic and copies ran while one was open for 5% of the time, Pallas kernels for 0%

profile of v1, /device:TPU:24, one launch (start us, length us, event | category | flops | bytes accessed | tf_op | source)
XLA Modules:
  0.0 203.5 jit_solution(1381720471441324296)
XLA Ops:
  7.7 7.8 %collective-permute-start = (f32[32,1,128]{2,0,1:T(8,128)S(1)}, f32[32,1,128]{2,0,1:T(8,128)S(1)}, u32[]{:S(2)}, u32[]{:S(2)}) collective-permute-start(f32[32,1,128]{2,0,1:T(8,128)S(1)} %bitcast.57), channel_id=1, source_target_pairs={{8,0},{16,8},{24,16},{32,24},{40,32},{48,40},{56,48},{64,56},{72,6... | collective-permute-start | bytes 49160 | tf_op jit(solution)/shard_map/ppermute | solution.py:17
  17.0 5.3 %collective-permute-done.1 = f32[32,1,128]{2,0,1:T(8,128)S(1)} collective-permute-done((f32[32,1,128]{2,0,1:T(8,128)S(1)}, f32[32,1,128]{2,0,1:T(8,128)S(1)}, u32[]{:S(2)}, u32[]{:S(2)}) %collective-permute-start.1) | collective-permute-done | bytes 16416 | tf_op jit(solution)/shard_map/ppermute | solution.py:16
  25.0 1.7 copy.63
  28.0 3.4 %collective-permute-start.3 = (f32[32,66,1]{1,0,2:T(8,128)S(1)}, f32[32,66,1]{1,0,2:T(8,128)S(1)}, u32[]{:S(2)}, u32[]{:S(2)}) collective-permute-start(f32[32,66,1]{1,0,2:T(8,128)S(1)} %copy.65), channel_id=1, source_target_pairs={{0,1},{1,2},{2,3},{3,4},{4,5},{5,6},{6,7},{7,0},{8,9},{9,10},{10,1... | collective-permute-start | bytes 25352 | tf_op jit(solution)/shard_map/ppermute | solution.py:16
  34.2 1.5 copy.66
  35.7 5.3 %fusion.7 = (f32[1,32,64,128]{3,2,1,0:T(8,128)S(1)}, f32[1,32,64,128]{3,2,1,0:T(8,128)S(1)}) fusion(f32[32,64,128]{2,1,0:T(8,128)} %param.10, f32[32,66,1]{2,1,0:T(8,128)} %copy.66, f32[32,1,128]{2,1,0:T(1,128)S(1)} %bitcast.51, f32[32,1,128]{2,1,0:T(1,128)S(1)} %bitcast.53, f32[32,66,1]{2,1,0:T(8,128)} %copy.64, f32[32,64,128]{2,1,0:T(8,128)} %param.11), kind=kLoop, calls=%fused_computation.20 | loop fusion | flops 5505024 | bytes 4243968 | tf_op jit(solution)/shard_map/stack | solution.py:92
  41.2 5.3 %collective-permute-start.5 = (f32[2,32,1,128]{3,1,2,0:T(8,128)S(1)}, f32[2,32,1,128]{3,1,2,0:T(8,128)S(1)}, u32[]{:S(2)}, u32[]{:S(2)}) collective-permute-start(f32[2,32,1,128]{3,1,2,0:T(8,128)S(1)} %bitcast.54), channel_id=1, source_target_pairs={{8,0},{16,8},{24,16},{32,24},{40,32},{48,40},{56,48},{64,56},{72,6... | collective-permute-start | bytes 98312 | tf_op jit(solution)/shard_map/ppermute | solution.py:17
  46.5 1.6 collective-permute-done.4
  48.5 2.9 %fusion.53 = (f32[2,32,66,1]{3,2,1,0:T(8,128)}, f32[2,32,66,1]{3,2,1,0:T(8,128)}) fusion(f32[2,32,66,128]{3,2,1,0:T(8,128)S(1)} %pad_maximum_fusion.1), kind=kLoop, calls=%fused_computation.90 | loop fusion | bytes 67584 | tf_op jit(solution)/shard_map/slice | solution.py:14
  51.3 2.4 %copy.71 = f32[2,32,66,1]{2,1,3,0:T(8,128)S(1)} copy(f32[2,32,66,1]{3,2,1,0:T(8,128)} %get-tuple-element.11) | data formatting | bytes 33792 | tf_op jit(solution)/shard_map/slice | solution.py:14
  53.8 3.2 %collective-permute-start.6 = (f32[2,32,66,1]{2,1,3,0:T(8,128)S(1)}, f32[2,32,66,1]{2,1,3,0:T(8,128)S(1)}, u32[]{:S(2)}, u32[]{:S(2)}) collective-permute-start(f32[2,32,66,1]{2,1,3,0:T(8,128)S(1)} %copy.71), channel_id=1, source_target_pairs={{0,1},{1,2},{2,3},{3,4},{4,5},{5,6},{6,7},{7,0},{8,9},{9,10},{10,1... | collective-permute-start | bytes 50696 | tf_op jit(solution)/shard_map/ppermute | solution.py:16
  57.0 2.4 %copy.72 = f32[2,32,66,1]{2,1,3,0:T(8,128)S(1)} copy(f32[2,32,66,1]{3,2,1,0:T(8,128)} %get-tuple-element.12) | data formatting | bytes 33792 | tf_op jit(solution)/shard_map/slice | solution.py:15
  59.7 2.3 %copy.73 = f32[2,32,66,1]{3,2,1,0:T(8,128)} copy(f32[2,32,66,1]{2,1,3,0:T(8,128)S(1)} %collective-permute-done.6) | data formatting | bytes 33792 | tf_op jit(solution)/shard_map/ppermute | solution.py:16
  61.9 3.7 %collective-permute-done.7 = f32[2,32,66,1]{2,1,3,0:T(8,128)S(1)} collective-permute-done((f32[2,32,66,1]{2,1,3,0:T(8,128)S(1)}, f32[2,32,66,1]{2,1,3,0:T(8,128)S(1)}, u32[]{:S(2)}, u32[]{:S(2)}) %collective-permute-start.7) | collective-permute-done | bytes 16928 | tf_op jit(solution)/shard_map/ppermute | solution.py:17
  65.7 2.3 %copy.74 = f32[2,32,66,1]{3,2,1,0:T(8,128)} copy(f32[2,32,66,1]{2,1,3,0:T(8,128)S(1)} %collective-permute-done.7) | data formatting | bytes 33792 | tf_op jit(solution)/shard_map/ppermute | solution.py:17
  68.0 5.2 %pad_maximum_fusion = f32[2,32,66,130]{3,2,1,0:T(8,128)S(1)} fusion(f32[2,32,66,1]{3,2,1,0:T(8,128)} %copy.74, f32[2,32,1,128]{3,2,1,0:T(1,128)S(1)} %bitcast.49, f32[1,32,64,128]{3,2,1,0:T(8,128)} %copy-done.1, f32[1,32,64,128]{3,2,1,0:T(8,128)S(1)} %get-tuple-element.21, f32[2,32,1,128]{3,2,1,0:T(1,128)S(1)} %bitcast.47, f32[2,32,66,1]{3,2,1,0:T(8,128)} %copy.73), kind=kLoop, calls=%fused_computation.2 | loop fusion | flops 2745600 | bytes 4392960 | tf_op jit(solution)/shard_map/concatenate | solution.py:18
  74.4 5.3 %convolution_bitcast_fusion.1 = f32[32,64,128]{2,1,0:T(8,128)} fusion(f32[32,64,64]{2,1,0:T(8,128)} %param.12, f32[32,64,128]{2,1,0:T(8,128)S(1)} %copy-done.2, f32[32,66,130]{2,1,0:T(8,128)S(1)} %get-tuple-element.10, f32[32,66,130]{2,1,0:T(8,128)S(1)} %get-tuple-element.9), kind=kOutput, calls=%fused_computation.14 | convolution fusion | flops 206831616 | bytes 13107200 | tf_op jit(solution)/shard_map/zij,zjn->zin/dot_general | solution.py:59
  81.6 1.6 gather_fusion
  83.1 75.9 %all-gather.2.cloned.1.call-done = f32[32,128,128]{2,0,1:T(8,128)} async-done(((f32[32,4,128]{2,0,1:T(8,128)}), f32[32,128,128]{2,0,1:T(8,128)}) %all-gather.2.cloned.1.call-update) | async-done | bytes 2097168 | tf_op jit(solution)/shard_map/all_gather | solution.py:63
  159.0 4.4 %fusion = f32[32,4,128]{2,1,0:T(4,128)S(1)} fusion(f32[32,128,128]{2,0,1:T(8,128)} %all-gather.2.cloned.1.call-done, f32[4,32,128]{2,0,1:T(4,128)S(1)} %gather_fusion, pred[4]{0:T(512)(128)(4,1)S(1)} %get-tuple-element.25), kind=kOutput, calls=%fused_computation.6 | convolution fusion | flops 25182208 | bytes 2228228 | tf_op jit(solution)/shard_map/zrk,zkn->zrn/dot_general | solution.py:67
  163.4 1.8 fusion.2
  165.3 4.1 %fusion.58 = f32[32,64,128]{2,1,0:T(8,128)S(1)} fusion(f32[32,64,128]{2,1,0:T(8,128)S(1)} %fusion.2, f32[32,128,128]{2,1,0:T(8,128)S(1)} %copy-done), kind=kOutput, calls=%fused_computation.96 | convolution fusion | flops 402653184 | bytes 4194304 | tf_op jit(solution)/shard_map/zij,zxj->zxi/dot_general | solution.py:73
  169.4 1.7 fusion.55
  171.1 1.6 copy.77
  172.7 1.6 copy.78
  175.2 2.3 %reshape.38 = f32[8,1,8192]{2,1,0:T(1,128)} reshape(f32[8,4,32,64]{3,2,1,0:T(8,128)} %broadcast_bitcast_fusion) | data formatting | bytes 524288
  177.5 4.8 %all-to-all-start = ((f32[8,1,8192]{2,1,0:T(1,128)}), f32[8,1,8192]{2,1,0:T(1,128)S(1)}, u32[]{:S(2)}, u32[]{:S(2)}) async-start(f32[8,1,8192]{2,1,0:T(1,128)} %reshape.38), calls=%async_computation | async-start | bytes 524288 | tf_op jit(solution)/shard_map/all_to_all | solution.py:78
  182.3 1.7 gather_fusion.1
  184.0 3.5 %all-to-all-done = f32[8,1,8192]{2,1,0:T(1,128)S(1)} async-done(((f32[8,1,8192]{2,1,0:T(1,128)}), f32[8,1,8192]{2,1,0:T(1,128)S(1)}, u32[]{:S(2)}, u32[]{:S(2)}) %all-to-all-start) | async-done | bytes 262176 | tf_op jit(solution)/shard_map/all_to_all | solution.py:78
  188.8 2.2 %reduce = f32[8,8192]{1,0:T(8,128)S(1)} reduce(f32[8,1,8192]{2,1,0:T(1,128)} %copy-done.4, f32[]{:T(128)} %broadcast.78), dimensions={1}, to_apply=%all_to_all.3.reduce_sub_computation | reduce | bytes 524292 | tf_op jit(solution)/shard_map/all_to_all | solution.py:78
  192.0 1.8 fusion.35
  193.9 2.8 %convolution_subtract_fusion = f32[32,64,128]{2,1,0:T(8,128)} fusion(f32[32,64,128]{2,1,0:T(8,128)S(1)} %fusion.58, f32[32,4,64]{2,1,0:T(4,128)S(1)} %fusion.35, f32[32,128,4]{1,2,0:T(4,128)S(1)} %copy-done.6), kind=kOutput, calls=%fused_computation.11 | convolution fusion | flops 12845056 | bytes 2195456 | tf_op jit(solution)/shard_map/zik,zkx->zxi/dot_general | solution.py:85
  (45 shorter events, 16.2 us)
Async XLA Ops:
  6.5 158.7 %copy-start = (f32[32,128,128]{2,1,0:T(8,128)S(1)}, f32[32,128,128]{2,1,0:T(8,128)}, u32[]{:S(2)}) copy-start(f32[32,128,128]{2,1,0:T(8,128)} %param.15) | copy-start | bytes 6291460
  6.5 152.5 %all-gather.2.cloned.1.call-start = ((), (), s32[]{:S(2)}) async-start(), calls=%async_computation.1 | async-start | bytes 2162688 | tf_op jit(solution)/shard_map/all_gather | solution.py:63
  7.7 9.3 %collective-permute-start = (f32[32,1,128]{2,0,1:T(8,128)S(1)}, f32[32,1,128]{2,0,1:T(8,128)S(1)}, u32[]{:S(2)}, u32[]{:S(2)}) collective-permute-start(f32[32,1,128]{2,0,1:T(8,128)S(1)} %bitcast.57), channel_id=1, source_target_pairs={{8,0},{16,8},{24,16},{32,24},{40,32},{48,40},{56,48},{64,56},{72,6... | collective-permute-start | bytes 49160 | tf_op jit(solution)/shard_map/ppermute | solution.py:17
  15.5 6.8 %collective-permute-start.1 = (f32[32,1,128]{2,0,1:T(8,128)S(1)}, f32[32,1,128]{2,0,1:T(8,128)S(1)}, u32[]{:S(2)}, u32[]{:S(2)}) collective-permute-start(f32[32,1,128]{2,0,1:T(8,128)S(1)} %bitcast.56), channel_id=1, source_target_pairs={{0,8},{8,16},{16,24},{24,32},{32,40},{40,48},{48,56},{56,64},{64,7... | collective-permute-start | bytes 49160 | tf_op jit(solution)/shard_map/ppermute | solution.py:16
  26.7 5.9 %collective-permute-start.2 = (f32[32,66,1]{1,0,2:T(8,128)S(1)}, f32[32,66,1]{1,0,2:T(8,128)S(1)}, u32[]{:S(2)}, u32[]{:S(2)}) collective-permute-start(f32[32,66,1]{1,0,2:T(8,128)S(1)} %copy.63), channel_id=1, source_target_pairs={{1,0},{2,1},{3,2},{4,3},{5,4},{6,5},{7,6},{0,7},{9,8},{10,9},{11,1... | collective-permute-start | bytes 25352 | tf_op jit(solution)/shard_map/ppermute | solution.py:17
  28.0 6.2 %collective-permute-start.3 = (f32[32,66,1]{1,0,2:T(8,128)S(1)}, f32[32,66,1]{1,0,2:T(8,128)S(1)}, u32[]{:S(2)}, u32[]{:S(2)}) collective-permute-start(f32[32,66,1]{1,0,2:T(8,128)S(1)} %copy.65), channel_id=1, source_target_pairs={{0,1},{1,2},{2,3},{3,4},{4,5},{5,6},{6,7},{7,0},{8,9},{9,10},{10,1... | collective-permute-start | bytes 25352 | tf_op jit(solution)/shard_map/ppermute | solution.py:16
  41.0 7.5 %copy-start.1 = (f32[1,32,64,128]{3,2,1,0:T(8,128)}, f32[1,32,64,128]{3,2,1,0:T(8,128)S(1)}, u32[]{:S(2)}) copy-start(f32[1,32,64,128]{3,2,1,0:T(8,128)S(1)} %get-tuple-element.22) | copy-start | bytes 3145732
  41.1 7.0 %collective-permute-start.4 = (f32[2,32,1,128]{3,1,2,0:T(8,128)S(1)}, f32[2,32,1,128]{3,1,2,0:T(8,128)S(1)}, u32[]{:S(2)}, u32[]{:S(2)}) collective-permute-start(f32[2,32,1,128]{3,1,2,0:T(8,128)S(1)} %bitcast.55), channel_id=1, source_target_pairs={{0,8},{8,16},{16,24},{24,32},{32,40},{40,48},{48,56},{56,64},{64,7... | collective-permute-start | bytes 98312 | tf_op jit(solution)/shard_map/ppermute | solution.py:16
  41.2 6.9 %collective-permute-start.5 = (f32[2,32,1,128]{3,1,2,0:T(8,128)S(1)}, f32[2,32,1,128]{3,1,2,0:T(8,128)S(1)}, u32[]{:S(2)}, u32[]{:S(2)}) collective-permute-start(f32[2,32,1,128]{3,1,2,0:T(8,128)S(1)} %bitcast.54), channel_id=1, source_target_pairs={{8,0},{16,8},{24,16},{32,24},{40,32},{48,40},{56,48},{64,56},{72,6... | collective-permute-start | bytes 98312 | tf_op jit(solution)/shard_map/ppermute | solution.py:17
  53.8 5.9 %collective-permute-start.6 = (f32[2,32,66,1]{2,1,3,0:T(8,128)S(1)}, f32[2,32,66,1]{2,1,3,0:T(8,128)S(1)}, u32[]{:S(2)}, u32[]{:S(2)}) collective-permute-start(f32[2,32,66,1]{2,1,3,0:T(8,128)S(1)} %copy.71), channel_id=1, source_target_pairs={{0,1},{1,2},{2,3},{3,4},{4,5},{5,6},{6,7},{7,0},{8,9},{9,10},{10,1... | collective-permute-start | bytes 50696 | tf_op jit(solution)/shard_map/ppermute | solution.py:16
  59.4 6.3 %collective-permute-start.7 = (f32[2,32,66,1]{2,1,3,0:T(8,128)S(1)}, f32[2,32,66,1]{2,1,3,0:T(8,128)S(1)}, u32[]{:S(2)}, u32[]{:S(2)}) collective-permute-start(f32[2,32,66,1]{2,1,3,0:T(8,128)S(1)} %copy.72), channel_id=1, source_target_pairs={{1,0},{2,1},{3,2},{4,3},{5,4},{6,5},{7,6},{0,7},{9,8},{10,9},{11,1... | collective-permute-start | bytes 50696 | tf_op jit(solution)/shard_map/ppermute | solution.py:17
  73.2 1.2 copy-start.2
  74.4 7.1 %copy-start.7 = (s32[4]{0:T(128)S(1)}, s32[4]{0:T(128)}, u32[]{:S(2)}) copy-start(s32[4]{0:T(128)} %constant.74.clone) | copy-start | bytes 52
  79.7 83.7 %copy-start.3 = (f32[32,64,128]{2,1,0:T(8,128)S(1)}, f32[32,64,128]{2,1,0:T(8,128)}, u32[]{:S(2)}) copy-start(f32[32,64,128]{2,1,0:T(8,128)} %convolution_bitcast_fusion.1) | copy-start | bytes 3145732
  79.7 83.7 %copy-start.5 = (f32[32,64,4]{1,2,0:T(4,128)S(1)}, f32[32,64,4]{1,2,0:T(4,128)}, u32[]{:S(2)}) copy-start(f32[32,64,4]{1,2,0:T(4,128)} %param.13) | copy-start | bytes 98308
  174.3 19.5 %copy-start.6 = (f32[32,128,4]{1,2,0:T(4,128)S(1)}, f32[32,128,4]{1,2,0:T(4,128)}, u32[]{:S(2)}) copy-start(f32[32,128,4]{1,2,0:T(4,128)} %param.16) | copy-start | bytes 196612
  177.5 10.0 %all-to-all-start = ((f32[8,1,8192]{2,1,0:T(1,128)}), f32[8,1,8192]{2,1,0:T(1,128)S(1)}, u32[]{:S(2)}, u32[]{:S(2)}) async-start(f32[8,1,8192]{2,1,0:T(1,128)} %reshape.38), calls=%async_computation | async-start | bytes 524288 | tf_op jit(solution)/shard_map/all_to_all | solution.py:78
  187.5 0.7 copy-start.4
Sparse Core Ops, SparseCore 0:
  81.6 77.3 all-gather.1
